TPU v7x, 256 devices: a whole 4x4x8 slice. The times are simulated.
256 devices in a mesh: row: 16 (over z, core), col: 16 (over x, y).
Axes of the slice: x: 4, y: 4, z: 8, core: 2. Of those that a mesh axis runs over, the one named last changes fastest.
Arguments:
- term_images: float32 [8, 4096, 4096], P(None, 'row', 'col'), may hold values from -6 to 6
- blur_width: float32 [8], replicated, may hold values from 0.8 to 6
- blur_coef: float32 [8], replicated, may hold values from -4 to 4
- direct_coef: float32 [8], replicated, may hold values from -1 to 1
- long_weight: float32 [8], replicated, may hold values from 0.2 to 2
- long_gain: float32 [1], replicated, may hold values from 0.5 to 1.5
- long_width: float32 [1], replicated, may hold values from 0.25 to 0.6
Outputs:
- resist_signal: float32 [4096, 4096], P('row', 'col')
All inputs are finite; a program needn't handle non-finite values.
Results may differ from a plain program's by a relative error of at most 0.00002.
Values sent between devices are 32-bit elements; how exact they have to be, the bound alone decides.
No kernel may reach another device: no remote copies, remote signals or barrier semaphores. Data moves between devices by JAX's collectives and lax.ppermute only.
A program may use at most 64 MiB of HBM per device.

v0:
```python
import jax
import jax.numpy as jnp
from jax import lax
from jax.sharding import PartitionSpec as P

REACH = 16
LEVELS = 5
RC = 8
BINOMIAL = (0.0625, 0.25, 0.375, 0.25, 0.0625)


def padded_2(cells, sides, width):
    for axis, dim in sides:
        count = lax.axis_size(axis)
        ends = count - 1
        head = lax.slice_in_dim(cells, 0, width, axis=dim)
        tail = lax.slice_in_dim(cells, cells.shape[dim] - width, cells.shape[dim], axis=dim)
        cells = jnp.concatenate(
            [
                lax.ppermute(tail, axis, [(i, (i + 1) % count) for i in range(ends)]),
                cells,
                lax.ppermute(head, axis, [((i + 1) % count, i) for i in range(ends)]),
            ],
            axis=dim,
        )
    return cells


def gauss_kernel(width, reach):
    offsets = jnp.arange(-reach, reach + 1).astype(jnp.float32)
    values = jnp.exp(-offsets * offsets / (2.0 * width[..., None] * width[..., None]))
    return values / jnp.sum(values, axis=-1, keepdims=True)


def down_pad(values, margin):
    return padded_2(values, (("row", 0), ("col", 1)), margin)


def up_pad(values, margin):
    return padded_2(values, (("row", 0), ("col", 1)), margin)


def coarse_pad(values, margin):
    return padded_2(values, (("row", 0), ("col", 1)), margin)


def coarsen(values, padder):
    row_count, col_count = values.shape
    padded = padder(values, 2)
    across = BINOMIAL[0] * padded[0:row_count, :]
    for tap_index in range(1, 5):
        across = across + BINOMIAL[tap_index] * padded[tap_index : tap_index + row_count, :]
    total = BINOMIAL[0] * across[:, 0:col_count]
    for tap_index in range(1, 5):
        total = total + BINOMIAL[tap_index] * across[:, tap_index : tap_index + col_count]
    return total[::2, ::2]


def refine(values, padder):
    row_count, col_count = values.shape
    padded = padder(values, 1)
    even_part = (padded[:-2] + 6.0 * padded[1:-1] + padded[2:]) * 0.125
    odd_part = (padded[1:-1] + padded[2:]) * 0.5
    rows_done = jnp.stack([even_part, odd_part], 1).reshape(2 * row_count, col_count + 2)
    even_part = (rows_done[:, :-2] + 6.0 * rows_done[:, 1:-1] + rows_done[:, 2:]) * 0.125
    odd_part = (rows_done[:, 1:-1] + rows_done[:, 2:]) * 0.5
    return jnp.stack([even_part, odd_part], 2).reshape(2 * row_count, 2 * col_count)


def coarse_blur(values, kernel, padder):
    row_count, col_count = values.shape
    padded = padder(values, RC)
    across = kernel[0] * padded[0:row_count, :]
    for tap_index in range(1, 2 * RC + 1):
        across = across + kernel[tap_index] * padded[tap_index : tap_index + row_count, :]
    total = kernel[0] * across[:, 0:col_count]
    for tap_index in range(1, 2 * RC + 1):
        total = total + kernel[tap_index] * across[:, tap_index : tap_index + col_count]
    return total


def taps_along(padded, kernel, axis, count):
    weights = kernel[:, :, None, None]
    total = weights[:, 0] * lax.slice_in_dim(padded, 0, count, axis=axis)
    for tap_index in range(1, 2 * REACH + 1):
        total = total + weights[:, tap_index] * lax.slice_in_dim(
            padded, tap_index, tap_index + count, axis=axis
        )
    return total


def on_device(term_images, blur_width, blur_coef, direct_coef, long_weight, long_gain, long_width):
    kernels = gauss_kernel(blur_width, REACH)
    tile_rows = term_images.shape[1]
    strips = lax.all_to_all(term_images, "col", split_axis=1, concat_axis=2, tiled=True)
    width_all = strips.shape[2]
    padded = jnp.pad(strips, ((0, 0), (0, 0), (REACH, REACH)))
    across_strips = taps_along(padded, kernels, 2, width_all)
    across = lax.all_to_all(across_strips, "col", split_axis=2, concat_axis=1, tiled=True)
    padded = padded_2(across, (("row", 1),), REACH)
    blurred = taps_along(padded, kernels, 1, tile_rows)
    local = jnp.sum(
        blur_coef[:, None, None] * blurred + direct_coef[:, None, None] * term_images, axis=0
    )
    source = jnp.sum(long_weight[:, None, None] * term_images * term_images, axis=0)
    coarse_kernel = gauss_kernel(long_width * RC, RC)[0]
    level_now = source
    for level_index in range(LEVELS):
        level_now = coarsen(level_now, down_pad)
    level_now = coarse_blur(level_now, coarse_kernel, coarse_pad)
    for level_index in range(LEVELS):
        level_now = refine(level_now, up_pad)
    return local + long_gain[0] * level_now


def solution(mesh):
    placed = (P(None, "row", "col"), P(), P(), P(), P(), P(), P())
    return jax.shard_map(
        on_device, mesh=mesh, in_specs=placed, out_specs=P("row", "col"), check_vma=False
    )
```

profile of v0, /device:TPU:134, one launch (start us, length us, event | category | flops | bytes accessed | tf_op | source)
XLA Modules:
  0.0 423.5 jit_solution(17075108637412598557)
XLA Ops:
  10.2 5.2 %collective-permute-start.5 = (f32[260,2]{1,0:T(8,128)S(1)}, f32[260,2]{1,0:T(8,128)S(1)}, u32[]{:S(2)}, u32[]{:S(2)}) collective-permute-start(f32[260,2]{1,0:T(8,128)S(1)} %get-tuple-element.8), channel_id=1, source_target_pairs={{1,0},{2,1},{3,2},{4,3},{5,4},{6,5},{7,6},{8,7},{9,8},{10,9},{11,1... | collective-permute-start | bytes 6248 | tf_op jit(solution)/shard_map/ppermute | solution.py:22
  19.9 8.1 %all-to-all-start = ((f32[8,256,256]{2,0,1:T(8,128)}), f32[8,256,256]{2,0,1:T(8,128)}, u32[]{:S(2)}, u32[]{:S(2)}) async-start(f32[8,256,256]{2,0,1:T(8,128)} %copy.171), calls=%async_computation | async-start | bytes 4194304 | tf_op jit(solution)/shard_map/all_to_all | solution.py:95
  39.2 4.9 %collective-permute-start.9 = (f32[132,2]{1,0:T(8,128)S(1)}, f32[132,2]{1,0:T(8,128)S(1)}, u32[]{:S(2)}, u32[]{:S(2)}) collective-permute-start(f32[132,2]{1,0:T(8,128)S(1)} %get-tuple-element.22), channel_id=1, source_target_pairs={{1,0},{2,1},{3,2},{4,3},{5,4},{6,5},{7,6},{8,7},{9,8},{10,9},{11,1... | collective-permute-start | bytes 3176 | tf_op jit(solution)/shard_map/ppermute | solution.py:22
  46.0 6.9 %collective-permute-done.9 = f32[132,2]{1,0:T(8,128)S(1)} collective-permute-done((f32[132,2]{1,0:T(8,128)S(1)}, f32[132,2]{1,0:T(8,128)S(1)}, u32[]{:S(2)}, u32[]{:S(2)}) %collective-permute-start.9) | collective-permute-done | bytes 1088 | tf_op jit(solution)/shard_map/ppermute | solution.py:22
  63.5 6.6 %collective-permute-start.13 = (f32[68,2]{1,0:T(8,128)S(1)}, f32[68,2]{1,0:T(8,128)S(1)}, u32[]{:S(2)}, u32[]{:S(2)}) collective-permute-start(f32[68,2]{1,0:T(8,128)S(1)} %get-tuple-element.34), channel_id=1, source_target_pairs={{1,0},{2,1},{3,2},{4,3},{5,4},{6,5},{7,6},{8,7},{9,8},{10,9},{11,1... | collective-permute-start | bytes 1640 | tf_op jit(solution)/shard_map/ppermute | solution.py:22
  72.1 5.9 %collective-permute-done.12 = f32[68,2]{1,0:T(8,128)S(1)} collective-permute-done((f32[68,2]{1,0:T(8,128)S(1)}, f32[68,2]{1,0:T(8,128)S(1)}, u32[]{:S(2)}, u32[]{:S(2)}) %collective-permute-start.12) | collective-permute-done | bytes 576 | tf_op jit(solution)/shard_map/ppermute | solution.py:20
  132.4 10.6 %fusion.192 = f32[8,24]{1,0:T(8,128)S(1)} fusion(f32[24,24]{1,0:T(8,128)S(1)} %pad_maximum_fusion.23, f32[]{:T(128)} %bitcast.59, f32[]{:T(128)} %bitcast.58, f32[]{:T(128)} %bitcast.57, f32[]{:T(128)} %bitcast.56, f32[]{:T(128)} %bitcast.55, f32[]{:T(128)} %bitcast.54, f32[]{:T(128)} %bitcast.53, f32[]{:T(128)} %bitcast.52, f32[]{:T(128)} %bitcast.51, ...), kind=kLoop, calls=%fused_computation.380 | loop fusion | flops 6336 | bytes 13892 | tf_op jit(solution)/shard_map/add | solution.py:75
  143.0 10.7 %multiply_add_fusion.1 = f32[8,8]{1,0:T(8,128)S(1)} fusion(f32[8,24]{1,0:T(8,128)S(1)} %fusion.192, f32[]{:T(128)} %bitcast.59, f32[]{:T(128)} %bitcast.58, f32[]{:T(128)} %bitcast.57, f32[]{:T(128)} %bitcast.56, f32[]{:T(128)} %bitcast.55, f32[]{:T(128)} %bitcast.54, f32[]{:T(128)} %bitcast.53, f32[]{:T(128)} %bitcast.52, f32[]{:T(128)} %bitcast.51, ...), kind=kLoop, calls=%fused_computation.413 | loop fusion | flops 2112 | bytes 4676 | tf_op jit(solution)/shard_map/add | solution.py:78
  192.6 4.9 %collective-permute-start.35 = (f32[1,32]{0,1:T(8,128)S(1)}, f32[1,32]{0,1:T(8,128)S(1)}, u32[]{:S(2)}, u32[]{:S(2)}) collective-permute-start(f32[1,32]{0,1:T(8,128)S(1)} %slice.1253), channel_id=1, source_target_pairs={{16,0},{32,16},{48,32},{64,48},{80,64},{96,80},{112,96},{128,112},... | collective-permute-start | bytes 392 | tf_op jit(solution)/shard_map/ppermute | solution.py:22
  208.7 4.1 copy.217
  215.6 46.7 %multiply_add_fusion = f32[8,16,4096]{2,1,0:T(8,128)} fusion(f32[8,16,4096]{2,1,0:T(8,128)} %all_to_all.29, f32[8]{0:T(128)S(1)} %get-tuple-element.48, f32[8]{0:T(128)S(1)} %get-tuple-element.49, f32[8]{0:T(128)S(1)} %get-tuple-element.50, f32[8]{0:T(128)S(1)} %get-tuple-element.51, f32[8]{0:T(128)S(1)} %get-tuple-element.52, f32[8]{0:T(128)S(1)} %get-tuple-element.53, ...), kind=kLoop, calls=%fused_computation.158 | loop fusion | flops 34078720 | bytes 4195360 | tf_op jit(solution)/shard_map/add | solution.py:86
  262.3 9.6 %copy.173 = f32[8,16,4096]{1,0,2:T(8,128)} copy(f32[8,16,4096]{2,1,0:T(8,128)} %multiply_add_fusion) | data formatting | bytes 4194304 | tf_op jit(solution)/shard_map/add | solution.py:86
  271.9 15.1 %reshape.234 = f32[16,1,32768]{2,1,0:T(1,128)} reshape(f32[4096,8,16]{2,1,0:T(8,128)} %bitcast.148) | data formatting | bytes 4194304
  287.0 4.5 %all-to-all-start.1 = ((f32[16,1,32768]{2,1,0:T(1,128)}), f32[16,1,32768]{2,1,0:T(1,128)}, u32[]{:S(2)}, u32[]{:S(2)}) async-start(f32[16,1,32768]{2,1,0:T(1,128)} %reshape.234), calls=%async_computation.1 | async-start | bytes 4194304 | tf_op jit(solution)/shard_map/all_to_all | solution.py:99
  301.8 4.5 %collective-permute-start.41 = (f32[66,1]{0,1:T(1,128)S(1)}, f32[66,1]{0,1:T(1,128)S(1)}, u32[]{:S(2)}, u32[]{:S(2)}) collective-permute-start(f32[66,1]{0,1:T(1,128)S(1)} %get-tuple-element.20), channel_id=1, source_target_pairs={{1,0},{2,1},{3,2},{4,3},{5,4},{6,5},{7,6},{8,7},{9,8},{10,9},{11,1... | collective-permute-start | bytes 800 | tf_op jit(solution)/shard_map/ppermute | solution.py:22
  308.2 6.6 %collective-permute-done.41 = f32[66,1]{0,1:T(1,128)S(1)} collective-permute-done((f32[66,1]{0,1:T(1,128)S(1)}, f32[66,1]{0,1:T(1,128)S(1)}, u32[]{:S(2)}, u32[]{:S(2)}) %collective-permute-start.41) | collective-permute-done | bytes 296 | tf_op jit(solution)/shard_map/ppermute | solution.py:22
  316.3 5.1 %collective-permute-start.43 = (f32[1,128]{0,1:T(8,128)S(1)}, f32[1,128]{0,1:T(8,128)S(1)}, u32[]{:S(2)}, u32[]{:S(2)}) collective-permute-start(f32[1,128]{0,1:T(8,128)S(1)} %slice.1255), channel_id=1, source_target_pairs={{16,0},{32,16},{48,32},{64,48},{80,64},{96,80},{112,96},{128,112},... | collective-permute-start | bytes 1544 | tf_op jit(solution)/shard_map/ppermute | solution.py:22
  327.8 4.4 %collective-permute-start.45 = (f32[130,1]{0,1:T(1,128)S(1)}, f32[130,1]{0,1:T(1,128)S(1)}, u32[]{:S(2)}, u32[]{:S(2)}) collective-permute-start(f32[130,1]{0,1:T(1,128)S(1)} %get-tuple-element.14), channel_id=1, source_target_pairs={{1,0},{2,1},{3,2},{4,3},{5,4},{6,5},{7,6},{8,7},{9,8},{10,9},{11,1... | collective-permute-start | bytes 1568 | tf_op jit(solution)/shard_map/ppermute | solution.py:22
  335.0 4.8 %collective-permute-done.44 = f32[130,1]{0,1:T(1,128)S(1)} collective-permute-done((f32[130,1]{0,1:T(1,128)S(1)}, f32[130,1]{0,1:T(1,128)S(1)}, u32[]{:S(2)}, u32[]{:S(2)}) %collective-permute-start.44) | collective-permute-done | bytes 552 | tf_op jit(solution)/shard_map/ppermute | solution.py:20
  340.9 8.6 %reduce.1 = f32[16,32768]{1,0:T(8,128)} reduce(f32[16,1,32768]{2,1,0:T(1,128)} %all-to-all-done.1, f32[]{:T(128)} %broadcast.217), dimensions={1}, to_apply=%all_to_all.30.reduce_sub_computation | reduce | bytes 4194308 | tf_op jit(solution)/shard_map/all_to_all | solution.py:99
  349.5 14.6 %reshape.235 = f32[4096,8,16]{2,1,0:T(8,128)} reshape(f32[16,32768]{1,0:T(8,128)} %reduce.1) | data formatting | bytes 4194304
  364.1 10.8 %copy.175 = f32[8,16,16,256]{3,2,1,0:T(8,128)} copy(f32[8,16,16,256]{2,0,3,1:T(8,128)} %bitcast.149) | data formatting | bytes 4194304 | tf_op jit(solution)/shard_map/all_to_all | solution.py:99
  381.2 4.2 collective-permute-done
  385.4 37.3 %fusion.7 = f32[256,256]{1,0:T(8,128)S(1)} fusion(f32[8,16,256]{2,1,0:T(8,128)S(1)} %collective-permute-done.1, f32[8,16,256]{2,1,0:T(8,128)S(1)} %collective-permute-done, f32[8,256,256]{2,1,0:T(8,128)} %bitcast.151, f32[8,256,256]{2,1,0:T(8,128)S(1)} %copy-done, f32[8]{0:T(128)S(1)} %copy-done.1, f32[8]{0:T(128)S(1)} %get-tuple-element.48, ...), kind=kLoop, calls=%fused_computation.38 | loop fusion | flops 52887552 | bytes 4719712 | tf_op jit(solution)/shard_map/reduce_sum | solution.py:102
  (213 shorter events, 176.6 us)
Async XLA Ops:
  10.2 17.8 %collective-permute-start.5 = (f32[260,2]{1,0:T(8,128)S(1)}, f32[260,2]{1,0:T(8,128)S(1)}, u32[]{:S(2)}, u32[]{:S(2)}) collective-permute-start(f32[260,2]{1,0:T(8,128)S(1)} %get-tuple-element.8), channel_id=1, source_target_pairs={{1,0},{2,1},{3,2},{4,3},{5,4},{6,5},{7,6},{8,7},{9,8},{10,9},{11,1... | collective-permute-start | bytes 6248 | tf_op jit(solution)/shard_map/ppermute | solution.py:22
  15.4 12.6 %collective-permute-start.4 = (f32[260,2]{1,0:T(8,128)S(1)}, f32[260,2]{1,0:T(8,128)S(1)}, u32[]{:S(2)}, u32[]{:S(2)}) collective-permute-start(f32[260,2]{1,0:T(8,128)S(1)} %get-tuple-element.7), channel_id=1, source_target_pairs={{0,1},{1,2},{2,3},{3,4},{4,5},{5,6},{6,7},{7,8},{8,9},{9,10},{10,1... | collective-permute-start | bytes 6248 | tf_op jit(solution)/shard_map/ppermute | solution.py:20
  19.9 188.8 %all-to-all-start = ((f32[8,256,256]{2,0,1:T(8,128)}), f32[8,256,256]{2,0,1:T(8,128)}, u32[]{:S(2)}, u32[]{:S(2)}) async-start(f32[8,256,256]{2,0,1:T(8,128)} %copy.171), calls=%async_computation | async-start | bytes 4194304 | tf_op jit(solution)/shard_map/all_to_all | solution.py:95
  39.2 13.7 %collective-permute-start.9 = (f32[132,2]{1,0:T(8,128)S(1)}, f32[132,2]{1,0:T(8,128)S(1)}, u32[]{:S(2)}, u32[]{:S(2)}) collective-permute-start(f32[132,2]{1,0:T(8,128)S(1)} %get-tuple-element.22), channel_id=1, source_target_pairs={{1,0},{2,1},{3,2},{4,3},{5,4},{6,5},{7,6},{8,7},{9,8},{10,9},{11,1... | collective-permute-start | bytes 3176 | tf_op jit(solution)/shard_map/ppermute | solution.py:22
  44.1 9.9 %collective-permute-start.8 = (f32[132,2]{1,0:T(8,128)S(1)}, f32[132,2]{1,0:T(8,128)S(1)}, u32[]{:S(2)}, u32[]{:S(2)}) collective-permute-start(f32[132,2]{1,0:T(8,128)S(1)} %get-tuple-element.21), channel_id=1, source_target_pairs={{0,1},{1,2},{2,3},{3,4},{4,5},{5,6},{6,7},{7,8},{8,9},{9,10},{10,1... | collective-permute-start | bytes 3176 | tf_op jit(solution)/shard_map/ppermute | solution.py:20
  63.5 8.7 %collective-permute-start.13 = (f32[68,2]{1,0:T(8,128)S(1)}, f32[68,2]{1,0:T(8,128)S(1)}, u32[]{:S(2)}, u32[]{:S(2)}) collective-permute-start(f32[68,2]{1,0:T(8,128)S(1)} %get-tuple-element.34), channel_id=1, source_target_pairs={{1,0},{2,1},{3,2},{4,3},{5,4},{6,5},{7,6},{8,7},{9,8},{10,9},{11,1... | collective-permute-start | bytes 1640 | tf_op jit(solution)/shard_map/ppermute | solution.py:22
  70.1 8.0 %collective-permute-start.12 = (f32[68,2]{1,0:T(8,128)S(1)}, f32[68,2]{1,0:T(8,128)S(1)}, u32[]{:S(2)}, u32[]{:S(2)}) collective-permute-start(f32[68,2]{1,0:T(8,128)S(1)} %get-tuple-element.33), channel_id=1, source_target_pairs={{0,1},{1,2},{2,3},{3,4},{4,5},{5,6},{6,7},{7,8},{8,9},{9,10},{10,1... | collective-permute-start | bytes 1640 | tf_op jit(solution)/shard_map/ppermute | solution.py:20
  88.5 7.8 %collective-permute-start.16 = (f32[36,2]{1,0:T(8,128)S(1)}, f32[36,2]{1,0:T(8,128)S(1)}, u32[]{:S(2)}, u32[]{:S(2)}) collective-permute-start(f32[36,2]{1,0:T(8,128)S(1)} %get-tuple-element.45), channel_id=1, source_target_pairs={{0,1},{1,2},{2,3},{3,4},{4,5},{5,6},{6,7},{7,8},{8,9},{9,10},{10,1... | collective-permute-start | bytes 872 | tf_op jit(solution)/shard_map/ppermute | solution.py:20
  106.7 7.7 %collective-permute-start.20 = (f32[20,2]{1,0:T(8,128)S(1)}, f32[20,2]{1,0:T(8,128)S(1)}, u32[]{:S(2)}, u32[]{:S(2)}) collective-permute-start(f32[20,2]{1,0:T(8,128)S(1)} %get-tuple-element.86), channel_id=1, source_target_pairs={{0,1},{1,2},{2,3},{3,4},{4,5},{5,6},{6,7},{7,8},{8,9},{9,10},{10,1... | collective-permute-start | bytes 488 | tf_op jit(solution)/shard_map/ppermute | solution.py:20
  122.7 6.6 %collective-permute-start.25 = (f32[24,8]{1,0:T(8,128)S(1)}, f32[24,8]{1,0:T(8,128)S(1)}, u32[]{:S(2)}, u32[]{:S(2)}) collective-permute-start(f32[24,8]{1,0:T(8,128)S(1)} %pad_maximum_fusion.22), channel_id=1, source_target_pairs={{1,0},{2,1},{3,2},{4,3},{5,4},{6,5},{7,6},{8,7},{9,8},{10,9},{11,1... | collective-permute-start | bytes 2312 | tf_op jit(solution)/shard_map/ppermute | solution.py:22
  124.6 7.7 %collective-permute-start.24 = (f32[24,8]{1,0:T(8,128)S(1)}, f32[24,8]{1,0:T(8,128)S(1)}, u32[]{:S(2)}, u32[]{:S(2)}) collective-permute-start(f32[24,8]{1,0:T(8,128)S(1)} %pad_maximum_fusion.22), channel_id=1, source_target_pairs={{0,1},{1,2},{2,3},{3,4},{4,5},{5,6},{6,7},{7,8},{8,9},{9,10},{10,1... | collective-permute-start | bytes 2312 | tf_op jit(solution)/shard_map/ppermute | solution.py:20
  163.8 7.7 %collective-permute-start.28 = (f32[10,1]{1,0:T(8,128)S(1)}, f32[10,1]{1,0:T(8,128)S(1)}, u32[]{:S(2)}, u32[]{:S(2)}) collective-permute-start(f32[10,1]{1,0:T(8,128)S(1)} %get-tuple-element.94), channel_id=1, source_target_pairs={{0,1},{1,2},{2,3},{3,4},{4,5},{5,6},{6,7},{7,8},{8,9},{9,10},{10,1... | collective-permute-start | bytes 128 | tf_op jit(solution)/shard_map/ppermute | solution.py:20
  172.1 8.3 %collective-permute-start.31 = (f32[1,16]{0,1:T(8,128)S(1)}, f32[1,16]{0,1:T(8,128)S(1)}, u32[]{:S(2)}, u32[]{:S(2)}) collective-permute-start(f32[1,16]{0,1:T(8,128)S(1)} %slice.1252), channel_id=1, source_target_pairs={{16,0},{32,16},{48,32},{64,48},{80,64},{96,80},{112,96},{128,112},... | collective-permute-start | bytes 200 | tf_op jit(solution)/shard_map/ppermute | solution.py:22
  182.4 7.6 %collective-permute-start.32 = (f32[18,1]{0,1:T(1,128)S(1)}, f32[18,1]{0,1:T(1,128)S(1)}, u32[]{:S(2)}, u32[]{:S(2)}) collective-permute-start(f32[18,1]{0,1:T(1,128)S(1)} %get-tuple-element.41), channel_id=1, source_target_pairs={{0,1},{1,2},{2,3},{3,4},{4,5},{5,6},{6,7},{7,8},{8,9},{9,10},{10,1... | collective-permute-start | bytes 224 | tf_op jit(solution)/shard_map/ppermute | solution.py:20
  190.6 6.9 %collective-permute-start.34 = (f32[1,32]{1,0:T(1,128)S(1)}, f32[1,32]{1,0:T(1,128)S(1)}, u32[]{:S(2)}, u32[]{:S(2)}) collective-permute-start(f32[1,32]{1,0:T(1,128)S(1)} %slice.1217), channel_id=1, source_target_pairs={{0,16},{16,32},{32,48},{48,64},{64,80},{80,96},{96,112},{112,128},... | collective-permute-start | bytes 392 | tf_op jit(solution)/shard_map/ppermute | solution.py:20
  200.9 7.6 %collective-permute-start.36 = (f32[34,1]{0,1:T(1,128)S(1)}, f32[34,1]{0,1:T(1,128)S(1)}, u32[]{:S(2)}, u32[]{:S(2)}) collective-permute-start(f32[34,1]{0,1:T(1,128)S(1)} %get-tuple-element.29), channel_id=1, source_target_pairs={{0,1},{1,2},{2,3},{3,4},{4,5},{5,6},{6,7},{7,8},{8,9},{9,10},{10,1... | collective-permute-start | bytes 416 | tf_op jit(solution)/shard_map/ppermute | solution.py:20
  287.0 53.4 %all-to-all-start.1 = ((f32[16,1,32768]{2,1,0:T(1,128)}), f32[16,1,32768]{2,1,0:T(1,128)}, u32[]{:S(2)}, u32[]{:S(2)}) async-start(f32[16,1,32768]{2,1,0:T(1,128)} %reshape.234), calls=%async_computation.1 | async-start | bytes 4194304 | tf_op jit(solution)/shard_map/all_to_all | solution.py:99
  291.8 9.9 %collective-permute-start.39 = (f32[1,64]{0,1:T(8,128)S(1)}, f32[1,64]{0,1:T(8,128)S(1)}, u32[]{:S(2)}, u32[]{:S(2)}) collective-permute-start(f32[1,64]{0,1:T(8,128)S(1)} %slice.1254), channel_id=1, source_target_pairs={{16,0},{32,16},{48,32},{64,48},{80,64},{96,80},{112,96},{128,112},... | collective-permute-start | bytes 776 | tf_op jit(solution)/shard_map/ppermute | solution.py:22
  301.8 13.0 %collective-permute-start.41 = (f32[66,1]{0,1:T(1,128)S(1)}, f32[66,1]{0,1:T(1,128)S(1)}, u32[]{:S(2)}, u32[]{:S(2)}) collective-permute-start(f32[66,1]{0,1:T(1,128)S(1)} %get-tuple-element.20), channel_id=1, source_target_pairs={{1,0},{2,1},{3,2},{4,3},{5,4},{6,5},{7,6},{8,7},{9,8},{10,9},{11,1... | collective-permute-start | bytes 800 | tf_op jit(solution)/shard_map/ppermute | solution.py:22
  306.3 9.4 %collective-permute-start.40 = (f32[66,1]{0,1:T(1,128)S(1)}, f32[66,1]{0,1:T(1,128)S(1)}, u32[]{:S(2)}, u32[]{:S(2)}) collective-permute-start(f32[66,1]{0,1:T(1,128)S(1)} %get-tuple-element.19), channel_id=1, source_target_pairs={{0,1},{1,2},{2,3},{3,4},{4,5},{5,6},{6,7},{7,8},{8,9},{9,10},{10,1... | collective-permute-start | bytes 800 | tf_op jit(solution)/shard_map/ppermute | solution.py:20
  316.3 11.5 %collective-permute-start.43 = (f32[1,128]{0,1:T(8,128)S(1)}, f32[1,128]{0,1:T(8,128)S(1)}, u32[]{:S(2)}, u32[]{:S(2)}) collective-permute-start(f32[1,128]{0,1:T(8,128)S(1)} %slice.1255), channel_id=1, source_target_pairs={{16,0},{32,16},{48,32},{64,48},{80,64},{96,80},{112,96},{128,112},... | collective-permute-start | bytes 1544 | tf_op jit(solution)/shard_map/ppermute | solution.py:22
  327.8 7.2 %collective-permute-start.45 = (f32[130,1]{0,1:T(1,128)S(1)}, f32[130,1]{0,1:T(1,128)S(1)}, u32[]{:S(2)}, u32[]{:S(2)}) collective-permute-start(f32[130,1]{0,1:T(1,128)S(1)} %get-tuple-element.14), channel_id=1, source_target_pairs={{1,0},{2,1},{3,2},{4,3},{5,4},{6,5},{7,6},{8,7},{9,8},{10,9},{11,1... | collective-permute-start | bytes 1568 | tf_op jit(solution)/shard_map/ppermute | solution.py:22
  332.2 7.6 %collective-permute-start.44 = (f32[130,1]{0,1:T(1,128)S(1)}, f32[130,1]{0,1:T(1,128)S(1)}, u32[]{:S(2)}, u32[]{:S(2)}) collective-permute-start(f32[130,1]{0,1:T(1,128)S(1)} %get-tuple-element.13), channel_id=1, source_target_pairs={{0,1},{1,2},{2,3},{3,4},{4,5},{5,6},{6,7},{7,8},{8,9},{9,10},{10,1... | collective-permute-start | bytes 1568 | tf_op jit(solution)/shard_map/ppermute | solution.py:20
  377.9 7.5 %collective-permute-start = (f32[8,16,256]{2,1,0:T(8,128)S(1)}, f32[8,16,256]{2,1,0:T(8,128)S(1)}, u32[]{:S(2)}, u32[]{:S(2)}) collective-permute-start(f32[8,16,256]{2,1,0:T(8,128)S(1)} %get-tuple-element.5), channel_id=1, source_target_pairs={{0,16},{16,32},{32,48},{48,64},{64,80},{80,96},{96,112},{112,128},... | collective-permute-start | bytes 393224 | tf_op jit(solution)/shard_map/ppermute | solution.py:20
  (28 other events, 180.0 us)
where the time goes:
time: 426 us; the launch traced here: 423 us
  starting transfers between devices  141 us (33%)
  other arithmetic  122 us (29%)
  waiting for transfers between devices  88.9 us (21%)
  local copies, waits for them, and re-layouts  68.9 us (16%)
    ppermute x23, waiting for transfers between devices, padded_2(): lax.ppermute(tail, axis, [(i, (i + 1) % count) for i in range(ends)])  74.1 us
    ppermute x23, starting transfers between devices, padded_2(): lax.ppermute(head, axis, [((i + 1) % count, i) for i in range(ends)])  68.1 us
    ppermute x23, starting transfers between devices, padded_2(): lax.ppermute(tail, axis, [(i, (i + 1) % count) for i in range(ends)])  60.8 us
    add x1, other arithmetic, taps_along(): total + weights[:, tap_index] * lax.slice_in_dim(padded, tap_index, tap_i...  46.7 us
    reduce_sum x1, other arithmetic, on_device(): jnp.sum(blur_coef[:, None, None] * blurred + direct_coef[:, None, None] *...  37.3 us
    unnamed x11, local copies, waits for them, and re-layouts  32.2 us
    ppermute x23, waiting for transfers between devices, padded_2(): lax.ppermute(head, axis, [((i + 1) % count, i) for i in range(ends)])  14.8 us
    all_to_all x2, local copies, waits for them, and re-layouts, on_device(): lax.all_to_all(across_strips, 'col', split_axis=2, concat_axis=1, tiled=T...  11.3 us
  transfers between devices with their start and end apart: 48, of which 24 were waited for; matrix products, arithmetic and copies ran while one was open for 9% of the time, Pallas kernels for 0%

commit v1 on v0

--- a/solution.py
+++ b/solution.py
@@ -92,7 +92,9 @@
 def on_device(term_images, blur_width, blur_coef, direct_coef, long_weight, long_gain, long_width):
     kernels = gauss_kernel(blur_width, REACH)
     tile_rows = term_images.shape[1]
-    strips = lax.all_to_all(term_images, "col", split_axis=1, concat_axis=2, tiled=True)
+    strips = jnp.concatenate(
+        lax.all_to_all(jnp.stack(jnp.split(term_images, lax.axis_size("col"), 1)), "col", 0, 0), 2
+    )
     width_all = strips.shape[2]
     padded = jnp.pad(strips, ((0, 0), (0, 0), (REACH, REACH)))
     across_strips = taps_along(padded, kernels, 2, width_all)

time: 426 us -> 400 us (0.939)
  other arithmetic: 122 us -> 94 us
    add x1, other arithmetic: 46.7 us -> 18.8 us  [taps_along(): total + weights[:, tap_index] * lax.slice_in_dim(padded, tap_index, tap_i...]
    unnamed x11 -> x25, local copies, waits for them, and re-layouts: 32.2 us -> 39.5 us
    all_to_all x2 -> x0, local copies, waits for them, and re-layouts: 6.89 us -> none  [on_device(): lax.all_to_all(term_images, 'col', split_axis=1, concat_axis=2, tiled=True)]
  transfers between devices with their start and end apart: 48 -> 48, of which waited for: 24 -> 23; matrix products, arithmetic and copies ran while one was open for 9% -> 11% of each run, Pallas kernels for 0% -> 0%
where the time goes in v1:
time: 400 us; the launch traced here: 397 us
  starting transfers between devices  141 us (35%)
  other arithmetic  94 us (24%)
  waiting for transfers between devices  87.7 us (22%)
  local copies, waits for them, and re-layouts  71.7 us (18%)
    ppermute x23, waiting for transfers between devices, padded_2(): lax.ppermute(tail, axis, [(i, (i + 1) % count) for i in range(ends)])  70.3 us
    ppermute x23, starting transfers between devices, padded_2(): lax.ppermute(head, axis, [((i + 1) % count, i) for i in range(ends)])  68.1 us
    ppermute x23, starting transfers between devices, padded_2(): lax.ppermute(tail, axis, [(i, (i + 1) % count) for i in range(ends)])  60.7 us
    unnamed x25, local copies, waits for them, and re-layouts  39.5 us
    reduce_sum x1, other arithmetic, on_device(): jnp.sum(blur_coef[:, None, None] * blurred + direct_coef[:, None, None] *...  37.3 us
    add x1, other arithmetic, taps_along(): total + weights[:, tap_index] * lax.slice_in_dim(padded, tap_index, tap_i...  18.8 us
    ppermute x23, waiting for transfers between devices, padded_2(): lax.ppermute(head, axis, [((i + 1) % count, i) for i in range(ends)])  17.4 us
    all_to_all x2, local copies, waits for them, and re-layouts, on_device(): lax.all_to_all(across_strips, 'col', split_axis=2, concat_axis=1, tiled=T...  11.3 us
  transfers between devices with their start and end apart: 48, of which 23 were waited for; matrix products, arithmetic and copies ran while one was open for 11% of the time, Pallas kernels for 0%

profile of v1, /device:TPU:134, one launch (start us, length us, event | category | flops | bytes accessed | tf_op | source)
XLA Modules:
  0.0 397.1 jit_solution(16357556742267504729)
XLA Ops:
  16.4 5.2 %collective-permute-start.5 = (f32[260,2]{1,0:T(8,128)S(1)}, f32[260,2]{1,0:T(8,128)S(1)}, u32[]{:S(2)}, u32[]{:S(2)}) collective-permute-start(f32[260,2]{1,0:T(8,128)S(1)} %get-tuple-element.8), channel_id=1, source_target_pairs={{1,0},{2,1},{3,2},{4,3},{5,4},{6,5},{7,6},{8,7},{9,8},{10,9},{11,1... | collective-permute-start | bytes 6248 | tf_op jit(solution)/shard_map/ppermute | solution.py:22
  24.2 8.1 %all-to-all-start = ((f32[16,8,16,256]{3,2,1,0:T(8,128)}), f32[16,8,16,256]{3,2,1,0:T(8,128)}, u32[]{:S(2)}, u32[]{:S(2)}) async-start(f32[16,8,16,256]{3,2,1,0:T(8,128)} %bitcast_dynamic-update-slice_fusion), calls=%async_computation | async-start | bytes 4194304 | tf_op jit(solution)/shard_map/all_to_all | solution.py:96
  40.5 4.1 %collective-permute-done.6 = f32[2,128]{1,0:T(2,128)S(1)} collective-permute-done((f32[2,128]{1,0:T(2,128)S(1)}, f32[2,128]{1,0:T(2,128)S(1)}, u32[]{:S(2)}, u32[]{:S(2)}) %collective-permute-start.6) | collective-permute-done | bytes 1056 | tf_op jit(solution)/shard_map/ppermute | solution.py:20
  44.8 4.9 %collective-permute-start.9 = (f32[132,2]{1,0:T(8,128)S(1)}, f32[132,2]{1,0:T(8,128)S(1)}, u32[]{:S(2)}, u32[]{:S(2)}) collective-permute-start(f32[132,2]{1,0:T(8,128)S(1)} %get-tuple-element.22), channel_id=1, source_target_pairs={{1,0},{2,1},{3,2},{4,3},{5,4},{6,5},{7,6},{8,7},{9,8},{10,9},{11,1... | collective-permute-start | bytes 3176 | tf_op jit(solution)/shard_map/ppermute | solution.py:22
  51.6 9.5 %collective-permute-done.9 = f32[132,2]{1,0:T(8,128)S(1)} collective-permute-done((f32[132,2]{1,0:T(8,128)S(1)}, f32[132,2]{1,0:T(8,128)S(1)}, u32[]{:S(2)}, u32[]{:S(2)}) %collective-permute-start.9) | collective-permute-done | bytes 1088 | tf_op jit(solution)/shard_map/ppermute | solution.py:22
  71.0 5.7 %collective-permute-start.13 = (f32[68,2]{1,0:T(8,128)S(1)}, f32[68,2]{1,0:T(8,128)S(1)}, u32[]{:S(2)}, u32[]{:S(2)}) collective-permute-start(f32[68,2]{1,0:T(8,128)S(1)} %get-tuple-element.34), channel_id=1, source_target_pairs={{1,0},{2,1},{3,2},{4,3},{5,4},{6,5},{7,6},{8,7},{9,8},{10,9},{11,1... | collective-permute-start | bytes 1640 | tf_op jit(solution)/shard_map/ppermute | solution.py:22
  78.8 5.9 %collective-permute-done.12 = f32[68,2]{1,0:T(8,128)S(1)} collective-permute-done((f32[68,2]{1,0:T(8,128)S(1)}, f32[68,2]{1,0:T(8,128)S(1)}, u32[]{:S(2)}, u32[]{:S(2)}) %collective-permute-start.12) | collective-permute-done | bytes 576 | tf_op jit(solution)/shard_map/ppermute | solution.py:20
  139.0 10.6 %fusion.192 = f32[8,24]{1,0:T(8,128)S(1)} fusion(f32[24,24]{1,0:T(8,128)S(1)} %pad_maximum_fusion.23, f32[]{:T(128)} %bitcast.74, f32[]{:T(128)} %bitcast.73, f32[]{:T(128)} %bitcast.72, f32[]{:T(128)} %bitcast.71, f32[]{:T(128)} %bitcast.70, f32[]{:T(128)} %bitcast.69, f32[]{:T(128)} %bitcast.68, f32[]{:T(128)} %bitcast.67, f32[]{:T(128)} %bitcast.66, ...), kind=kLoop, calls=%fused_computation.395 | loop fusion | flops 6336 | bytes 13892 | tf_op jit(solution)/shard_map/add | solution.py:75
  149.7 10.7 %multiply_add_fusion.1 = f32[8,8]{1,0:T(8,128)S(1)} fusion(f32[8,24]{1,0:T(8,128)S(1)} %fusion.192, f32[]{:T(128)} %bitcast.74, f32[]{:T(128)} %bitcast.73, f32[]{:T(128)} %bitcast.72, f32[]{:T(128)} %bitcast.71, f32[]{:T(128)} %bitcast.70, f32[]{:T(128)} %bitcast.69, f32[]{:T(128)} %bitcast.68, f32[]{:T(128)} %bitcast.67, f32[]{:T(128)} %bitcast.66, ...), kind=kLoop, calls=%fused_computation.428 | loop fusion | flops 2112 | bytes 4676 | tf_op jit(solution)/shard_map/add | solution.py:78
  199.2 4.9 %collective-permute-start.35 = (f32[1,32]{0,1:T(8,128)S(1)}, f32[1,32]{0,1:T(8,128)S(1)}, u32[]{:S(2)}, u32[]{:S(2)}) collective-permute-start(f32[1,32]{0,1:T(8,128)S(1)} %slice.1253), channel_id=1, source_target_pairs={{16,0},{32,16},{48,32},{64,48},{80,64},{96,80},{112,96},{128,112},... | collective-permute-start | bytes 392 | tf_op jit(solution)/shard_map/ppermute | solution.py:22
  217.2 18.8 %multiply_add_fusion = f32[8,16,4096]{2,1,0:T(8,128)} fusion(f32[8,16,4096]{2,1,0:T(8,128)S(1)} %bitcast.181, f32[8]{0:T(128)S(1)} %get-tuple-element.48, f32[8]{0:T(128)S(1)} %get-tuple-element.49, f32[8]{0:T(128)S(1)} %get-tuple-element.50, f32[8]{0:T(128)S(1)} %get-tuple-element.51, f32[8]{0:T(128)S(1)} %get-tuple-element.52, ...), kind=kLoop, calls=%fused_computation.157 | loop fusion | flops 34078720 | bytes 4195360 | tf_op jit(solution)/shard_map/add | solution.py:86
  235.9 9.6 %copy.170 = f32[8,16,4096]{1,0,2:T(8,128)} copy(f32[8,16,4096]{2,1,0:T(8,128)} %multiply_add_fusion) | data formatting | bytes 4194304 | tf_op jit(solution)/shard_map/add | solution.py:86
  245.5 15.1 %reshape.242 = f32[16,1,32768]{2,1,0:T(1,128)} reshape(f32[4096,8,16]{2,1,0:T(8,128)} %bitcast.177) | data formatting | bytes 4194304
  260.6 4.5 %all-to-all-start.1 = ((f32[16,1,32768]{2,1,0:T(1,128)}), f32[16,1,32768]{2,1,0:T(1,128)}, u32[]{:S(2)}, u32[]{:S(2)}) async-start(f32[16,1,32768]{2,1,0:T(1,128)} %reshape.242), calls=%async_computation.1 | async-start | bytes 4194304 | tf_op jit(solution)/shard_map/all_to_all | solution.py:101
  275.4 4.5 %collective-permute-start.41 = (f32[66,1]{0,1:T(1,128)S(1)}, f32[66,1]{0,1:T(1,128)S(1)}, u32[]{:S(2)}, u32[]{:S(2)}) collective-permute-start(f32[66,1]{0,1:T(1,128)S(1)} %get-tuple-element.20), channel_id=1, source_target_pairs={{1,0},{2,1},{3,2},{4,3},{5,4},{6,5},{7,6},{8,7},{9,8},{10,9},{11,1... | collective-permute-start | bytes 800 | tf_op jit(solution)/shard_map/ppermute | solution.py:22
  281.8 6.6 %collective-permute-done.41 = f32[66,1]{0,1:T(1,128)S(1)} collective-permute-done((f32[66,1]{0,1:T(1,128)S(1)}, f32[66,1]{0,1:T(1,128)S(1)}, u32[]{:S(2)}, u32[]{:S(2)}) %collective-permute-start.41) | collective-permute-done | bytes 296 | tf_op jit(solution)/shard_map/ppermute | solution.py:22
  289.9 5.1 %collective-permute-start.43 = (f32[1,128]{0,1:T(8,128)S(1)}, f32[1,128]{0,1:T(8,128)S(1)}, u32[]{:S(2)}, u32[]{:S(2)}) collective-permute-start(f32[1,128]{0,1:T(8,128)S(1)} %slice.1255), channel_id=1, source_target_pairs={{16,0},{32,16},{48,32},{64,48},{80,64},{96,80},{112,96},{128,112},... | collective-permute-start | bytes 1544 | tf_op jit(solution)/shard_map/ppermute | solution.py:22
  301.4 4.4 %collective-permute-start.45 = (f32[130,1]{0,1:T(1,128)S(1)}, f32[130,1]{0,1:T(1,128)S(1)}, u32[]{:S(2)}, u32[]{:S(2)}) collective-permute-start(f32[130,1]{0,1:T(1,128)S(1)} %get-tuple-element.14), channel_id=1, source_target_pairs={{1,0},{2,1},{3,2},{4,3},{5,4},{6,5},{7,6},{8,7},{9,8},{10,9},{11,1... | collective-permute-start | bytes 1568 | tf_op jit(solution)/shard_map/ppermute | solution.py:22
  308.6 4.8 %collective-permute-done.44 = f32[130,1]{0,1:T(1,128)S(1)} collective-permute-done((f32[130,1]{0,1:T(1,128)S(1)}, f32[130,1]{0,1:T(1,128)S(1)}, u32[]{:S(2)}, u32[]{:S(2)}) %collective-permute-start.44) | collective-permute-done | bytes 552 | tf_op jit(solution)/shard_map/ppermute | solution.py:20
  314.5 8.6 %reduce.1 = f32[16,32768]{1,0:T(8,128)} reduce(f32[16,1,32768]{2,1,0:T(1,128)} %all-to-all-done.1, f32[]{:T(128)} %broadcast.217), dimensions={1}, to_apply=%all_to_all.17.reduce_sub_computation | reduce | bytes 4194308 | tf_op jit(solution)/shard_map/all_to_all | solution.py:101
  323.1 14.6 %reshape.243 = f32[4096,8,16]{2,1,0:T(8,128)} reshape(f32[16,32768]{1,0:T(8,128)} %reduce.1) | data formatting | bytes 4194304
  337.7 10.8 %copy.172 = f32[8,16,16,256]{3,2,1,0:T(8,128)} copy(f32[8,16,16,256]{2,0,3,1:T(8,128)} %bitcast.178) | data formatting | bytes 4194304 | tf_op jit(solution)/shard_map/all_to_all | solution.py:101
  354.8 4.2 %collective-permute-done = f32[8,16,256]{2,1,0:T(8,128)S(1)} collective-permute-done((f32[8,16,256]{2,1,0:T(8,128)S(1)}, f32[8,16,256]{2,1,0:T(8,128)S(1)}, u32[]{:S(2)}, u32[]{:S(2)}) %collective-permute-start) | collective-permute-done | bytes 131104 | tf_op jit(solution)/shard_map/ppermute | solution.py:20
  359.0 37.3 %fusion.7 = f32[256,256]{1,0:T(8,128)S(1)} fusion(f32[8,16,256]{2,1,0:T(8,128)S(1)} %collective-permute-done.1, f32[8,16,256]{2,1,0:T(8,128)S(1)} %collective-permute-done, f32[8,256,256]{2,1,0:T(8,128)} %bitcast.180, f32[8,256,256]{2,1,0:T(8,128)S(1)} %copy-done, f32[8]{0:T(128)S(1)} %copy-done.1, f32[8]{0:T(128)S(1)} %get-tuple-element.48, ...), kind=kLoop, calls=%fused_computation.38 | loop fusion | flops 52887552 | bytes 4719712 | tf_op jit(solution)/shard_map/reduce_sum | solution.py:104
  (227 shorter events, 176.5 us)
Async XLA Ops:
  2.1 14.2 %collective-permute-start.3 = (f32[2,256]{1,0:T(2,128)S(1)}, f32[2,256]{1,0:T(2,128)S(1)}, u32[]{:S(2)}, u32[]{:S(2)}) collective-permute-start(f32[2,256]{1,0:T(2,128)S(1)} %get-tuple-element.12), channel_id=1, source_target_pairs={{16,0},{32,16},{48,32},{64,48},{80,64},{96,80},{112,96},{128,112},... | collective-permute-start | bytes 6152 | tf_op jit(solution)/shard_map/ppermute | solution.py:22
  4.0 12.3 %collective-permute-start.2 = (f32[2,256]{1,0:T(2,128)S(1)}, f32[2,256]{1,0:T(2,128)S(1)}, u32[]{:S(2)}, u32[]{:S(2)}) collective-permute-start(f32[2,256]{1,0:T(2,128)S(1)} %get-tuple-element.11), channel_id=1, source_target_pairs={{0,16},{16,32},{32,48},{48,64},{64,80},{80,96},{96,112},{112,128},... | collective-permute-start | bytes 6152 | tf_op jit(solution)/shard_map/ppermute | solution.py:20
  16.4 15.9 %collective-permute-start.5 = (f32[260,2]{1,0:T(8,128)S(1)}, f32[260,2]{1,0:T(8,128)S(1)}, u32[]{:S(2)}, u32[]{:S(2)}) collective-permute-start(f32[260,2]{1,0:T(8,128)S(1)} %get-tuple-element.8), channel_id=1, source_target_pairs={{1,0},{2,1},{3,2},{4,3},{5,4},{6,5},{7,6},{8,7},{9,8},{10,9},{11,1... | collective-permute-start | bytes 6248 | tf_op jit(solution)/shard_map/ppermute | solution.py:22
  21.6 10.7 %collective-permute-start.4 = (f32[260,2]{1,0:T(8,128)S(1)}, f32[260,2]{1,0:T(8,128)S(1)}, u32[]{:S(2)}, u32[]{:S(2)}) collective-permute-start(f32[260,2]{1,0:T(8,128)S(1)} %get-tuple-element.7), channel_id=1, source_target_pairs={{0,1},{1,2},{2,3},{3,4},{4,5},{5,6},{6,7},{7,8},{8,9},{9,10},{10,1... | collective-permute-start | bytes 6248 | tf_op jit(solution)/shard_map/ppermute | solution.py:20
  24.2 191.2 %all-to-all-start = ((f32[16,8,16,256]{3,2,1,0:T(8,128)}), f32[16,8,16,256]{3,2,1,0:T(8,128)}, u32[]{:S(2)}, u32[]{:S(2)}) async-start(f32[16,8,16,256]{3,2,1,0:T(8,128)} %bitcast_dynamic-update-slice_fusion), calls=%async_computation | async-start | bytes 4194304 | tf_op jit(solution)/shard_map/all_to_all | solution.py:96
  44.8 16.3 %collective-permute-start.9 = (f32[132,2]{1,0:T(8,128)S(1)}, f32[132,2]{1,0:T(8,128)S(1)}, u32[]{:S(2)}, u32[]{:S(2)}) collective-permute-start(f32[132,2]{1,0:T(8,128)S(1)} %get-tuple-element.22), channel_id=1, source_target_pairs={{1,0},{2,1},{3,2},{4,3},{5,4},{6,5},{7,6},{8,7},{9,8},{10,9},{11,1... | collective-permute-start | bytes 3176 | tf_op jit(solution)/shard_map/ppermute | solution.py:22
  49.6 12.3 %collective-permute-start.8 = (f32[132,2]{1,0:T(8,128)S(1)}, f32[132,2]{1,0:T(8,128)S(1)}, u32[]{:S(2)}, u32[]{:S(2)}) collective-permute-start(f32[132,2]{1,0:T(8,128)S(1)} %get-tuple-element.21), channel_id=1, source_target_pairs={{0,1},{1,2},{2,3},{3,4},{4,5},{5,6},{6,7},{7,8},{8,9},{9,10},{10,1... | collective-permute-start | bytes 3176 | tf_op jit(solution)/shard_map/ppermute | solution.py:20
  71.0 7.7 %collective-permute-start.13 = (f32[68,2]{1,0:T(8,128)S(1)}, f32[68,2]{1,0:T(8,128)S(1)}, u32[]{:S(2)}, u32[]{:S(2)}) collective-permute-start(f32[68,2]{1,0:T(8,128)S(1)} %get-tuple-element.34), channel_id=1, source_target_pairs={{1,0},{2,1},{3,2},{4,3},{5,4},{6,5},{7,6},{8,7},{9,8},{10,9},{11,1... | collective-permute-start | bytes 1640 | tf_op jit(solution)/shard_map/ppermute | solution.py:22
  76.7 8.0 %collective-permute-start.12 = (f32[68,2]{1,0:T(8,128)S(1)}, f32[68,2]{1,0:T(8,128)S(1)}, u32[]{:S(2)}, u32[]{:S(2)}) collective-permute-start(f32[68,2]{1,0:T(8,128)S(1)} %get-tuple-element.33), channel_id=1, source_target_pairs={{0,1},{1,2},{2,3},{3,4},{4,5},{5,6},{6,7},{7,8},{8,9},{9,10},{10,1... | collective-permute-start | bytes 1640 | tf_op jit(solution)/shard_map/ppermute | solution.py:20
  95.2 7.8 %collective-permute-start.16 = (f32[36,2]{1,0:T(8,128)S(1)}, f32[36,2]{1,0:T(8,128)S(1)}, u32[]{:S(2)}, u32[]{:S(2)}) collective-permute-start(f32[36,2]{1,0:T(8,128)S(1)} %get-tuple-element.45), channel_id=1, source_target_pairs={{0,1},{1,2},{2,3},{3,4},{4,5},{5,6},{6,7},{7,8},{8,9},{9,10},{10,1... | collective-permute-start | bytes 872 | tf_op jit(solution)/shard_map/ppermute | solution.py:20
  113.3 7.7 %collective-permute-start.20 = (f32[20,2]{1,0:T(8,128)S(1)}, f32[20,2]{1,0:T(8,128)S(1)}, u32[]{:S(2)}, u32[]{:S(2)}) collective-permute-start(f32[20,2]{1,0:T(8,128)S(1)} %get-tuple-element.86), channel_id=1, source_target_pairs={{0,1},{1,2},{2,3},{3,4},{4,5},{5,6},{6,7},{7,8},{8,9},{9,10},{10,1... | collective-permute-start | bytes 488 | tf_op jit(solution)/shard_map/ppermute | solution.py:20
  131.2 7.7 %collective-permute-start.24 = (f32[24,8]{1,0:T(8,128)S(1)}, f32[24,8]{1,0:T(8,128)S(1)}, u32[]{:S(2)}, u32[]{:S(2)}) collective-permute-start(f32[24,8]{1,0:T(8,128)S(1)} %pad_maximum_fusion.22), channel_id=1, source_target_pairs={{0,1},{1,2},{2,3},{3,4},{4,5},{5,6},{6,7},{7,8},{8,9},{9,10},{10,1... | collective-permute-start | bytes 2312 | tf_op jit(solution)/shard_map/ppermute | solution.py:20
  170.4 7.7 %collective-permute-start.28 = (f32[10,1]{1,0:T(8,128)S(1)}, f32[10,1]{1,0:T(8,128)S(1)}, u32[]{:S(2)}, u32[]{:S(2)}) collective-permute-start(f32[10,1]{1,0:T(8,128)S(1)} %get-tuple-element.94), channel_id=1, source_target_pairs={{0,1},{1,2},{2,3},{3,4},{4,5},{5,6},{6,7},{7,8},{8,9},{9,10},{10,1... | collective-permute-start | bytes 128 | tf_op jit(solution)/shard_map/ppermute | solution.py:20
  178.7 8.3 %collective-permute-start.31 = (f32[1,16]{0,1:T(8,128)S(1)}, f32[1,16]{0,1:T(8,128)S(1)}, u32[]{:S(2)}, u32[]{:S(2)}) collective-permute-start(f32[1,16]{0,1:T(8,128)S(1)} %slice.1252), channel_id=1, source_target_pairs={{16,0},{32,16},{48,32},{64,48},{80,64},{96,80},{112,96},{128,112},... | collective-permute-start | bytes 200 | tf_op jit(solution)/shard_map/ppermute | solution.py:22
  189.0 7.6 %collective-permute-start.32 = (f32[18,1]{0,1:T(1,128)S(1)}, f32[18,1]{0,1:T(1,128)S(1)}, u32[]{:S(2)}, u32[]{:S(2)}) collective-permute-start(f32[18,1]{0,1:T(1,128)S(1)} %get-tuple-element.41), channel_id=1, source_target_pairs={{0,1},{1,2},{2,3},{3,4},{4,5},{5,6},{6,7},{7,8},{8,9},{9,10},{10,1... | collective-permute-start | bytes 224 | tf_op jit(solution)/shard_map/ppermute | solution.py:20
  207.5 7.6 %collective-permute-start.36 = (f32[34,1]{0,1:T(1,128)S(1)}, f32[34,1]{0,1:T(1,128)S(1)}, u32[]{:S(2)}, u32[]{:S(2)}) collective-permute-start(f32[34,1]{0,1:T(1,128)S(1)} %get-tuple-element.29), channel_id=1, source_target_pairs={{0,1},{1,2},{2,3},{3,4},{4,5},{5,6},{6,7},{7,8},{8,9},{9,10},{10,1... | collective-permute-start | bytes 416 | tf_op jit(solution)/shard_map/ppermute | solution.py:20
  260.6 53.4 %all-to-all-start.1 = ((f32[16,1,32768]{2,1,0:T(1,128)}), f32[16,1,32768]{2,1,0:T(1,128)}, u32[]{:S(2)}, u32[]{:S(2)}) async-start(f32[16,1,32768]{2,1,0:T(1,128)} %reshape.242), calls=%async_computation.1 | async-start | bytes 4194304 | tf_op jit(solution)/shard_map/all_to_all | solution.py:101
  265.4 9.9 %collective-permute-start.39 = (f32[1,64]{0,1:T(8,128)S(1)}, f32[1,64]{0,1:T(8,128)S(1)}, u32[]{:S(2)}, u32[]{:S(2)}) collective-permute-start(f32[1,64]{0,1:T(8,128)S(1)} %slice.1254), channel_id=1, source_target_pairs={{16,0},{32,16},{48,32},{64,48},{80,64},{96,80},{112,96},{128,112},... | collective-permute-start | bytes 776 | tf_op jit(solution)/shard_map/ppermute | solution.py:22
  275.4 13.0 %collective-permute-start.41 = (f32[66,1]{0,1:T(1,128)S(1)}, f32[66,1]{0,1:T(1,128)S(1)}, u32[]{:S(2)}, u32[]{:S(2)}) collective-permute-start(f32[66,1]{0,1:T(1,128)S(1)} %get-tuple-element.20), channel_id=1, source_target_pairs={{1,0},{2,1},{3,2},{4,3},{5,4},{6,5},{7,6},{8,7},{9,8},{10,9},{11,1... | collective-permute-start | bytes 800 | tf_op jit(solution)/shard_map/ppermute | solution.py:22
  279.9 9.4 %collective-permute-start.40 = (f32[66,1]{0,1:T(1,128)S(1)}, f32[66,1]{0,1:T(1,128)S(1)}, u32[]{:S(2)}, u32[]{:S(2)}) collective-permute-start(f32[66,1]{0,1:T(1,128)S(1)} %get-tuple-element.19), channel_id=1, source_target_pairs={{0,1},{1,2},{2,3},{3,4},{4,5},{5,6},{6,7},{7,8},{8,9},{9,10},{10,1... | collective-permute-start | bytes 800 | tf_op jit(solution)/shard_map/ppermute | solution.py:20
  289.9 11.5 %collective-permute-start.43 = (f32[1,128]{0,1:T(8,128)S(1)}, f32[1,128]{0,1:T(8,128)S(1)}, u32[]{:S(2)}, u32[]{:S(2)}) collective-permute-start(f32[1,128]{0,1:T(8,128)S(1)} %slice.1255), channel_id=1, source_target_pairs={{16,0},{32,16},{48,32},{64,48},{80,64},{96,80},{112,96},{128,112},... | collective-permute-start | bytes 1544 | tf_op jit(solution)/shard_map/ppermute | solution.py:22
  301.4 7.2 %collective-permute-start.45 = (f32[130,1]{0,1:T(1,128)S(1)}, f32[130,1]{0,1:T(1,128)S(1)}, u32[]{:S(2)}, u32[]{:S(2)}) collective-permute-start(f32[130,1]{0,1:T(1,128)S(1)} %get-tuple-element.14), channel_id=1, source_target_pairs={{1,0},{2,1},{3,2},{4,3},{5,4},{6,5},{7,6},{8,7},{9,8},{10,9},{11,1... | collective-permute-start | bytes 1568 | tf_op jit(solution)/shard_map/ppermute | solution.py:22
  305.8 7.6 %collective-permute-start.44 = (f32[130,1]{0,1:T(1,128)S(1)}, f32[130,1]{0,1:T(1,128)S(1)}, u32[]{:S(2)}, u32[]{:S(2)}) collective-permute-start(f32[130,1]{0,1:T(1,128)S(1)} %get-tuple-element.13), channel_id=1, source_target_pairs={{0,1},{1,2},{2,3},{3,4},{4,5},{5,6},{6,7},{7,8},{8,9},{9,10},{10,1... | collective-permute-start | bytes 1568 | tf_op jit(solution)/shard_map/ppermute | solution.py:20
  351.5 7.5 %collective-permute-start = (f32[8,16,256]{2,1,0:T(8,128)S(1)}, f32[8,16,256]{2,1,0:T(8,128)S(1)}, u32[]{:S(2)}, u32[]{:S(2)}) collective-permute-start(f32[8,16,256]{2,1,0:T(8,128)S(1)} %get-tuple-element.5), channel_id=1, source_target_pairs={{0,16},{16,32},{32,48},{48,64},{64,80},{80,96},{96,112},{112,128},... | collective-permute-start | bytes 393224 | tf_op jit(solution)/shard_map/ppermute | solution.py:20
  (28 other events, 173.7 us)
